TPU v7x, 512 devices: a whole 4x8x8 slice. The times are simulated.
512 devices in a mesh: sp: 64 (over z_hi, y, core), ch: 8 (over z_lo, x).
Axes of the slice: x: 4, y: 8, z: 8 (z_hi: 4, z_lo: 2; z = z_hi * 2 + z_lo), core: 2. Of those that a mesh axis runs over, the one named last changes fastest.
Arguments:
- image: bfloat16 [64, 4, 64, 768], P('sp', None, None, 'ch'), may hold values from -60 to 60
- cotangent: bfloat16 [64, 4, 64, 768], P('sp', None, None, 'ch'), may hold values from -6 to 6
- kernel: bfloat16 [7, 7, 768], P(None, None, 'ch'), may hold values from -0.875 to 0.875
- w_in: bfloat16 [768, 3072], P(None, 'ch'), may hold values from -0.21875 to 0.21875
- w_out: bfloat16 [3072, 768], P('ch'), may hold values from -0.109375 to 0.109375
Outputs:
- output: bfloat16 [64, 4, 64, 768], P('sp', None, None, 'ch')
- grad_image: bfloat16 [64, 4, 64, 768], P('sp', None, None, 'ch')
- grad_in: float32 [768, 3072], P(None, 'ch')
- grad_out: float32 [3072, 768], P('ch')
- grad_kernel: float32 [7, 7, 768], P(None, None, 'ch')
All inputs are finite; a program needn't handle non-finite values.
Results may differ from a plain program's by a relative error of at most 0.015.
Values may be sent and summed in bfloat16 or wider, within the bound.
A program may use at most 64 MiB of HBM per device.

v0:
```python
import jax
import jax.numpy as jnp
from jax import lax
from jax.sharding import PartitionSpec as P

GRID_W = 8


def passed_along(block, axis, distance):
    devices = range(lax.axis_size(axis))
    route = [(i - distance, i) for i in devices if i - distance in devices]
    return lax.ppermute(block, axis, route)


def from_peer(piece, offset):
    return passed_along(piece, "sp", offset)


def widen(block):
    column = lax.axis_index("sp") % GRID_W
    left = from_peer(block[:, -3:], 1)
    left = jnp.where(column == 0, jnp.zeros_like(left), left)
    right = from_peer(block[:, :3], -1)
    right = jnp.where(column == GRID_W - 1, jnp.zeros_like(right), right)
    wide = jnp.concatenate([left, block, right], axis=1)
    upper = from_peer(wide[-3:], GRID_W)
    lower = from_peer(wide[:3], -GRID_W)
    return jnp.concatenate([upper, wide, lower], axis=0)


def shards(image, cotangent, kernel, w_in, w_out):
    block = image[0]
    grad_map = cotangent[0]
    rows, cols, panel = block.shape
    chans = w_in.shape[0]
    kernel_f = kernel.astype(jnp.float32)
    padded = widen(block).astype(jnp.float32)
    total = jnp.zeros((rows, cols, panel), jnp.float32)
    for row in range(7):
        for col in range(7):
            total = total + kernel_f[row, col] * padded[row : row + rows, col : col + cols]
    conv = total.astype(jnp.bfloat16)
    conv_f = conv.astype(jnp.float32)
    first_sum, square_sum = lax.psum(
        (jnp.sum(conv_f, axis=-1, keepdims=True), jnp.sum(conv_f * conv_f, axis=-1, keepdims=True)),
        "ch",
    )
    mean = first_sum / chans
    var = square_sum / chans - mean * mean
    rstd = lax.rsqrt(var + 1e-06)
    normed_all = lax.all_gather(
        ((conv_f - mean) * rstd).astype(jnp.bfloat16), "ch", axis=2, tiled=True
    )
    local_hat = (conv_f - mean) * rstd
    pre = jnp.einsum("hwc,cf->hwf", normed_all, w_in, preferred_element_type=jnp.float32)
    act = (0.5 * pre * (1.0 + jax.scipy.special.erf(pre / jnp.sqrt(2.0)))).astype(jnp.bfloat16)
    partial_out = jnp.einsum("hwf,fc->hwc", act, w_out, preferred_element_type=jnp.float32).astype(
        jnp.bfloat16
    )
    branch = lax.psum_scatter(partial_out, "ch", scatter_dimension=2, tiled=True).astype(
        jnp.float32
    )
    output = (block.astype(jnp.float32) + branch).astype(jnp.bfloat16)
    grad_all = lax.all_gather(grad_map, "ch", axis=2, tiled=True)
    d_act = jnp.einsum("hwc,fc->hwf", grad_all, w_out, preferred_element_type=jnp.float32)
    grad_out = jnp.einsum("hwf,hwc->fc", act, grad_all, preferred_element_type=jnp.float32)
    slope = 0.5 * (1.0 + jax.scipy.special.erf(pre / jnp.sqrt(2.0))) + pre * jnp.exp(
        -0.5 * pre * pre
    ) / jnp.sqrt(2.0 * jnp.pi)
    d_pre = (d_act * slope).astype(jnp.bfloat16)
    grad_in = jnp.einsum("hwc,hwf->cf", normed_all, d_pre, preferred_element_type=jnp.float32)
    partial_norm = jnp.einsum(
        "hwf,cf->hwc", d_pre, w_in, preferred_element_type=jnp.float32
    ).astype(jnp.bfloat16)
    d_norm = lax.psum_scatter(partial_norm, "ch", scatter_dimension=2, tiled=True).astype(
        jnp.float32
    )
    first, second = lax.psum(
        (
            jnp.sum(d_norm, axis=-1, keepdims=True),
            jnp.sum(d_norm * local_hat, axis=-1, keepdims=True),
        ),
        "ch",
    )
    d_conv = (rstd * (d_norm - first / chans - local_hat * second / chans)).astype(jnp.bfloat16)
    d_conv_f = d_conv.astype(jnp.float32)
    taps = []
    for row in range(7):
        for col in range(7):
            taps.append(jnp.sum(d_conv_f * padded[row : row + rows, col : col + cols], axis=(0, 1)))
    grad_kernel = jnp.stack(taps).reshape(7, 7, panel)
    d_padded = widen(d_conv).astype(jnp.float32)
    back = grad_map.astype(jnp.float32)
    for row in range(7):
        for col in range(7):
            back = (
                back
                + kernel_f[row, col] * d_padded[6 - row : 6 - row + rows, 6 - col : 6 - col + cols]
            )
    grad_image = back.astype(jnp.bfloat16)
    grad_in, grad_out, grad_kernel = lax.psum((grad_in, grad_out, grad_kernel), "sp")
    return (output[None], grad_image[None], grad_in, grad_out, grad_kernel)


def solution(mesh):
    return jax.shard_map(
        shards,
        mesh=mesh,
        in_specs=(
            P("sp", None, None, "ch"),
            P("sp", None, None, "ch"),
            P(None, None, "ch"),
            P(None, "ch"),
            P("ch", None),
        ),
        out_specs=(
            P("sp", None, None, "ch"),
            P("sp", None, None, "ch"),
            P(None, "ch"),
            P("ch", None),
            P(None, None, "ch"),
        ),
        check_vma=False,
    )
```

profile of v0, /device:TPU:6, one launch (start us, length us, event | category | flops | bytes accessed | tf_op | source)
XLA Modules:
  0.0 716.1 jit_solution(15601981577770408222)
XLA Ops:
  8.1 1.0 copy.38
  9.2 1.7 collective-permute-start
  10.9 1.3 collective-permute-start.1
  12.2 0.7 convert_element_type.55
  13.4 0.6 slice_bitcast_fusion.46
  14.0 1.0 copy.42
  15.0 0.5 collective-permute-done.1
  15.9 11.0 %collective-permute-start.2 = (bf16[3,70,96]{1,0,2:T(4,128)(2,1)S(1)}, bf16[3,70,96]{1,0,2:T(4,128)(2,1)S(1)}, u32[]{:S(2)}, u32[]{:S(2)}) collective-permute-start(bf16[3,70,96]{1,0,2:T(4,128)(2,1)S(1)} %get-tuple-element.85), channel_id=1, source_target_pairs={{0,64},{8,72},{16,80},{24,88},{32,96},{40,104},{48,112},{56,120},{... | collective-permute-start | bytes 120968 | tf_op jit(solution)/shard_map/ppermute | solution.py:12
  26.9 1.3 collective-permute-start.3
  28.2 29.8 %all-gather = bf16[1,4,64,768]{2,1,0,3:T(4,128)(2,1)S(1)} all-gather(bf16[1,4,64,96]{2,1,0,3:T(4,128)(2,1)S(1)} %copy.42), channel_id=2, replica_groups=mesh['sp'=64,'ch'=8] {'ch'}, dimensions={3}, use_global_device_ids=true | all-gather | bytes 442368 | tf_op jit(solution)/shard_map/all_gather | solution.py:64
  58.0 0.5 copy.43
  58.6 0.7 maximum_convert_fusion
  59.6 12.5 %convert_reduce_fusion.1 = (f32[4,64]{1,0:T(4,128)S(1)}, f32[4,64]{1,0:T(4,128)S(1)}, bf16[4,64,96]{1,0,2:T(4,128)(2,1)S(1)}) fusion(f32[10,70,96]{1,0,2:T(8,128)S(1)} %maximum_convert_fusion, f32[96]{0:T(128)S(1)} %get-tuple-element.90, f32[96]{0:T(128)S(1)} %get-tuple-element.91, f32[96]{0:T(128)S(1)} %get-tuple-element.92, f32[96]{0:T(128)S(1)} %get-tuple-element.93, ...), kind=kLoop, calls=%fused_computation.76 | loop fusion | flops 2506240 | bytes 4886912 | tf_op jit(solution)/shard_map/reduce_sum | solution.py:45
  72.1 16.1 %all-reduce.2 = (f32[4,64,1]{1,0,2:T(4,128)S(1)}, f32[4,64,1]{1,0,2:T(4,128)S(1)}) all-reduce(f32[4,64,1]{1,0,2:T(4,128)S(1)} %bitcast.206, f32[4,64,1]{1,0,2:T(4,128)S(1)} %bitcast.205), channel_id=1, replica_groups=mesh['sp'=64,'ch'=8] {'ch'}, use_global_device_ids=true, to_apply=%region_3.4 | all-reduce | flops 512 | bytes 4096 | tf_op jit(solution)/shard_map/psum | solution.py:44
  88.4 29.7 %all_gather.6 = bf16[4,64,768]{1,0,2:T(4,128)(2,1)S(1)} all-gather(bf16[4,64,96]{1,0,2:T(4,128)(2,1)S(1)} %fusion.14), channel_id=1, replica_groups=mesh['sp'=64,'ch'=8] {'ch'}, dimensions={2}, use_global_device_ids=true | all-gather | bytes 442368 | tf_op jit(solution)/shard_map/all_gather | solution.py:51
  118.1 0.5 copy.39
  118.7 0.4 fusion.4
  119.0 0.7 copy-done.6
  119.7 0.4 fusion
  120.1 0.7 copy-done.4
  120.8 0.4 convolution_convert_fusion
  121.2 0.6 copy.50
  121.8 1.2 reshape.23
  123.1 1.4 convolution_convert_fusion.1
  124.5 0.6 copy.48
  125.1 1.2 reshape.21
  126.6 1.4 convolution_bitcast_fusion.1
  128.0 1.4 convolution_bitcast_fusion
  129.4 43.3 %reduce-scatter.9.cloned.1.call-done = bf16[96,256]{1,0:T(8,128)(2,1)} async-done(((bf16[768,256]{1,0:T(8,128)(2,1)}), bf16[96,256]{1,0:T(8,128)(2,1)}) %reduce-scatter.9.cloned.1.call-update) | async-done | bytes 49168
  172.7 0.9 reshape.24
  173.8 16.5 %all-reduce.1 = (f32[4,64]{1,0:T(4,128)S(1)}, f32[4,64,1]{1,0,2:T(4,128)S(1)}) all-reduce(f32[4,64]{1,0:T(4,128)S(1)} %get-tuple-element.70, f32[4,64,1]{1,0,2:T(4,128)S(1)} %bitcast.204), channel_id=1, replica_groups=mesh['sp'=64,'ch'=8] {'ch'}, use_global_device_ids=true, to_apply=%region_9.10 | all-reduce | flops 512 | bytes 4096 | tf_op jit(solution)/shard_map/psum | solution.py:78
  190.3 6.9 fusion.68
  197.2 4.6 fusion.67
  201.9 1.5 collective-permute-start.4
  203.5 6.7 fusion.69
  210.2 1.3 collective-permute-start.5
  211.5 7.1 reduce-scatter.7.cloned.1.call-done
  218.6 0.9 reshape.22
  220.3 6.4 collective-permute-start.6
  226.7 1.3 collective-permute-start.7
  228.1 0.7 copy.46
  229.0 282.1 %psum.55 = f32[7,7,96]{2,1,0:T(8,128)} all-reduce(f32[7,7,96]{2,1,0:T(8,128)S(1)} %reshape.13), channel_id=1, replica_groups=mesh['sp'=64,'ch'=8] {'sp'}, use_global_device_ids=true, to_apply=%region_61.62 | all-reduce | flops 4704 | bytes 37632 | tf_op jit(solution)/shard_map/psum | solution.py:101
  511.1 0.7 maximum_convert_fusion.1
  512.1 12.5 %fusion.121 = bf16[1,4,64,96]{2,1,3,0:T(4,128)(2,1)S(1)} fusion(f32[10,70,96]{1,0,2:T(8,128)S(1)} %maximum_convert_fusion.1, f32[96]{0:T(128)S(1)} %copy-done.45, f32[96]{0:T(128)S(1)} %copy-done.47, f32[96]{0:T(128)S(1)} %copy-done.49, f32[96]{0:T(128)S(1)} %copy-done.51, f32[96]{0:T(128)S(1)} %copy-done.53, f32[96]{0:T(128)S(1)} %copy-done.55, ...), kind=kLoop, calls=%fused_computation.243 | loop fusion | flops 2457600 | bytes 4934016 | tf_op jit(solution)/shard_map/broadcast_in_dim | solution.py:102
  524.6 0.7 copy.47
  525.3 179.9 %all-reduce.5.cloned.1.call-done = (f32[768,384]{1,0:T(8,128)}, f32[384,768]{1,0:T(8,128)}) async-done(((f32[768,384]{1,0:T(8,128)}, f32[384,768]{1,0:T(8,128)}), (f32[768,384]{1,0:T(8,128)}, f32[384,768]{1,0:T(8,128)})) %all-reduce.5.cloned.1.call-update) | async-done | bytes 2359312 | tf_op jit(solution)/shard_map/psum | solution.py:101
  705.2 2.5 copy.54
  707.6 1.0 copy.55
  (199 shorter events, 2.2 us)
Async XLA Ops:
  8.0 164.7 %reduce-scatter.9.cloned.1.call-start = ((), (), s32[]{:S(2)}) async-start(), calls=%async_computation.3 | async-start | bytes 442368
  9.2 5.8 collective-permute-start
  10.9 4.6 collective-permute-start.1
  15.9 42.7 %collective-permute-start.2 = (bf16[3,70,96]{1,0,2:T(4,128)(2,1)S(1)}, bf16[3,70,96]{1,0,2:T(4,128)(2,1)S(1)}, u32[]{:S(2)}, u32[]{:S(2)}) collective-permute-start(bf16[3,70,96]{1,0,2:T(4,128)(2,1)S(1)} %get-tuple-element.85), channel_id=1, source_target_pairs={{0,64},{8,72},{16,80},{24,88},{32,96},{40,104},{48,112},{56,120},{... | collective-permute-start | bytes 120968 | tf_op jit(solution)/shard_map/ppermute | solution.py:12
  26.9 31.7 %collective-permute-start.3 = (bf16[3,70,96]{1,0,2:T(4,128)(2,1)S(1)}, bf16[3,70,96]{1,0,2:T(4,128)(2,1)S(1)}, u32[]{:S(2)}, u32[]{:S(2)}) collective-permute-start(bf16[3,70,96]{1,0,2:T(4,128)(2,1)S(1)} %get-tuple-element.86), channel_id=1, source_target_pairs={{64,0},{72,8},{80,16},{88,24},{96,32},{104,40},{112,48},{120,56},{... | collective-permute-start | bytes 120968 | tf_op jit(solution)/shard_map/ppermute | solution.py:12
  123.0 95.5 %reduce-scatter.7.cloned.1.call-start = ((), (), s32[]{:S(2)}) async-start(), calls=%async_computation.2 | async-start | bytes 442368
  126.4 578.8 %all-reduce.5.cloned.1.call-start = ((), (), s32[]{:S(2)}) async-start(), calls=%async_computation.4 | async-start | bytes 4718592 | tf_op jit(solution)/shard_map/psum | solution.py:101
  201.9 17.5 %collective-permute-start.4 = (bf16[4,3,96]{1,0,2:T(4,128)(2,1)S(1)}, bf16[4,3,96]{1,0,2:T(4,128)(2,1)S(1)}, u32[]{:S(2)}, u32[]{:S(2)}) collective-permute-start(bf16[4,3,96]{1,0,2:T(4,128)(2,1)S(1)} %get-tuple-element.83), channel_id=1, source_target_pairs={{0,8},{8,16},{16,24},{24,32},{32,40},{40,48},{48,56},{56,64},{64,7... | collective-permute-start | bytes 6920 | tf_op jit(solution)/shard_map/ppermute | solution.py:12
  210.2 9.4 %collective-permute-start.5 = (bf16[4,3,96]{1,0,2:T(4,128)(2,1)S(1)}, bf16[4,3,96]{1,0,2:T(4,128)(2,1)S(1)}, u32[]{:S(2)}, u32[]{:S(2)}) collective-permute-start(bf16[4,3,96]{1,0,2:T(4,128)(2,1)S(1)} %get-tuple-element.84), channel_id=1, source_target_pairs={{8,0},{16,8},{24,16},{32,24},{40,32},{48,40},{56,48},{64,56},{72,6... | collective-permute-start | bytes 6920 | tf_op jit(solution)/shard_map/ppermute | solution.py:12
  219.8 291.9 %copy-start.9 = (f32[96]{0:T(128)S(1)}, f32[96]{0:T(128)}, u32[]{:S(2)}) copy-start(f32[96]{0:T(128)} %copy-done.8) | copy-start | bytes 1156
  219.8 291.9 %copy-start.11 = (f32[96]{0:T(128)S(1)}, f32[96]{0:T(128)}, u32[]{:S(2)}) copy-start(f32[96]{0:T(128)} %copy-done.10) | copy-start | bytes 1156
  219.8 291.9 %copy-start.13 = (f32[96]{0:T(128)S(1)}, f32[96]{0:T(128)}, u32[]{:S(2)}) copy-start(f32[96]{0:T(128)} %copy-done.12) | copy-start | bytes 1156
  219.9 291.9 %copy-start.15 = (f32[96]{0:T(128)S(1)}, f32[96]{0:T(128)}, u32[]{:S(2)}) copy-start(f32[96]{0:T(128)} %copy-done.14) | copy-start | bytes 1156
  219.9 291.9 %copy-start.17 = (f32[96]{0:T(128)S(1)}, f32[96]{0:T(128)}, u32[]{:S(2)}) copy-start(f32[96]{0:T(128)} %copy-done.16) | copy-start | bytes 1156
  219.9 291.9 %copy-start.19 = (f32[96]{0:T(128)S(1)}, f32[96]{0:T(128)}, u32[]{:S(2)}) copy-start(f32[96]{0:T(128)} %copy-done.18) | copy-start | bytes 1156
  219.9 291.9 %copy-start.21 = (f32[96]{0:T(128)S(1)}, f32[96]{0:T(128)}, u32[]{:S(2)}) copy-start(f32[96]{0:T(128)} %copy-done.20) | copy-start | bytes 1156
  219.9 291.9 %copy-start.23 = (f32[96]{0:T(128)S(1)}, f32[96]{0:T(128)}, u32[]{:S(2)}) copy-start(f32[96]{0:T(128)} %copy-done.22) | copy-start | bytes 1156
  219.9 291.9 %copy-start.25 = (f32[96]{0:T(128)S(1)}, f32[96]{0:T(128)}, u32[]{:S(2)}) copy-start(f32[96]{0:T(128)} %copy-done.24) | copy-start | bytes 1156
  219.9 291.9 %copy-start.27 = (f32[96]{0:T(128)S(1)}, f32[96]{0:T(128)}, u32[]{:S(2)}) copy-start(f32[96]{0:T(128)} %copy-done.26) | copy-start | bytes 1156
  219.9 291.9 %copy-start.29 = (f32[96]{0:T(128)S(1)}, f32[96]{0:T(128)}, u32[]{:S(2)}) copy-start(f32[96]{0:T(128)} %copy-done.28) | copy-start | bytes 1156
  219.9 291.9 %copy-start.31 = (f32[96]{0:T(128)S(1)}, f32[96]{0:T(128)}, u32[]{:S(2)}) copy-start(f32[96]{0:T(128)} %copy-done.30) | copy-start | bytes 1156
  219.9 291.9 %copy-start.33 = (f32[96]{0:T(128)S(1)}, f32[96]{0:T(128)}, u32[]{:S(2)}) copy-start(f32[96]{0:T(128)} %copy-done.32) | copy-start | bytes 1156
  220.0 291.9 %copy-start.35 = (f32[96]{0:T(128)S(1)}, f32[96]{0:T(128)}, u32[]{:S(2)}) copy-start(f32[96]{0:T(128)} %copy-done.34) | copy-start | bytes 1156
  220.0 291.9 %copy-start.37 = (f32[96]{0:T(128)S(1)}, f32[96]{0:T(128)}, u32[]{:S(2)}) copy-start(f32[96]{0:T(128)} %copy-done.36) | copy-start | bytes 1156
  220.0 291.9 %copy-start.39 = (f32[96]{0:T(128)S(1)}, f32[96]{0:T(128)}, u32[]{:S(2)}) copy-start(f32[96]{0:T(128)} %copy-done.38) | copy-start | bytes 1156
  220.0 291.9 %copy-start.41 = (f32[96]{0:T(128)S(1)}, f32[96]{0:T(128)}, u32[]{:S(2)}) copy-start(f32[96]{0:T(128)} %copy-done.40) | copy-start | bytes 1156
  220.0 291.9 %copy-start.43 = (f32[96]{0:T(128)S(1)}, f32[96]{0:T(128)}, u32[]{:S(2)}) copy-start(f32[96]{0:T(128)} %copy-done.42) | copy-start | bytes 1156
  220.0 291.9 %copy-start.45 = (f32[96]{0:T(128)S(1)}, f32[96]{0:T(128)}, u32[]{:S(2)}) copy-start(f32[96]{0:T(128)} %copy-done.44) | copy-start | bytes 1156
  220.0 291.9 %copy-start.47 = (f32[96]{0:T(128)S(1)}, f32[96]{0:T(128)}, u32[]{:S(2)}) copy-start(f32[96]{0:T(128)} %copy-done.46) | copy-start | bytes 1156
  220.0 291.9 %copy-start.49 = (f32[96]{0:T(128)S(1)}, f32[96]{0:T(128)}, u32[]{:S(2)}) copy-start(f32[96]{0:T(128)} %copy-done.48) | copy-start | bytes 1156
  220.0 291.9 %copy-start.51 = (f32[96]{0:T(128)S(1)}, f32[96]{0:T(128)}, u32[]{:S(2)}) copy-start(f32[96]{0:T(128)} %copy-done.50) | copy-start | bytes 1156
  220.0 291.9 %copy-start.53 = (f32[96]{0:T(128)S(1)}, f32[96]{0:T(128)}, u32[]{:S(2)}) copy-start(f32[96]{0:T(128)} %copy-done.52) | copy-start | bytes 1156
  220.1 291.9 %copy-start.55 = (f32[96]{0:T(128)S(1)}, f32[96]{0:T(128)}, u32[]{:S(2)}) copy-start(f32[96]{0:T(128)} %copy-done.54) | copy-start | bytes 1156
  220.1 291.9 %copy-start.57 = (f32[96]{0:T(128)S(1)}, f32[96]{0:T(128)}, u32[]{:S(2)}) copy-start(f32[96]{0:T(128)} %copy-done.56) | copy-start | bytes 1156
  220.1 291.9 %copy-start.59 = (f32[96]{0:T(128)S(1)}, f32[96]{0:T(128)}, u32[]{:S(2)}) copy-start(f32[96]{0:T(128)} %copy-done.58) | copy-start | bytes 1156
  220.1 291.9 %copy-start.61 = (f32[96]{0:T(128)S(1)}, f32[96]{0:T(128)}, u32[]{:S(2)}) copy-start(f32[96]{0:T(128)} %copy-done.60) | copy-start | bytes 1156
  220.1 291.9 %copy-start.63 = (f32[96]{0:T(128)S(1)}, f32[96]{0:T(128)}, u32[]{:S(2)}) copy-start(f32[96]{0:T(128)} %copy-done.62) | copy-start | bytes 1156
  220.1 291.9 %copy-start.65 = (f32[96]{0:T(128)S(1)}, f32[96]{0:T(128)}, u32[]{:S(2)}) copy-start(f32[96]{0:T(128)} %copy-done.64) | copy-start | bytes 1156
  220.1 291.9 %copy-start.67 = (f32[96]{0:T(128)S(1)}, f32[96]{0:T(128)}, u32[]{:S(2)}) copy-start(f32[96]{0:T(128)} %copy-done.66) | copy-start | bytes 1156
  220.1 291.9 %copy-start.69 = (f32[96]{0:T(128)S(1)}, f32[96]{0:T(128)}, u32[]{:S(2)}) copy-start(f32[96]{0:T(128)} %copy-done.68) | copy-start | bytes 1156
  220.1 291.9 %copy-start.71 = (f32[96]{0:T(128)S(1)}, f32[96]{0:T(128)}, u32[]{:S(2)}) copy-start(f32[96]{0:T(128)} %copy-done.70) | copy-start | bytes 1156
  220.1 291.9 %copy-start.73 = (f32[96]{0:T(128)S(1)}, f32[96]{0:T(128)}, u32[]{:S(2)}) copy-start(f32[96]{0:T(128)} %copy-done.72) | copy-start | bytes 1156
  220.2 291.9 %copy-start.75 = (f32[96]{0:T(128)S(1)}, f32[96]{0:T(128)}, u32[]{:S(2)}) copy-start(f32[96]{0:T(128)} %copy-done.74) | copy-start | bytes 1156
  220.2 291.9 %copy-start.77 = (f32[96]{0:T(128)S(1)}, f32[96]{0:T(128)}, u32[]{:S(2)}) copy-start(f32[96]{0:T(128)} %copy-done.76) | copy-start | bytes 1156
  220.2 291.9 %copy-start.79 = (f32[96]{0:T(128)S(1)}, f32[96]{0:T(128)}, u32[]{:S(2)}) copy-start(f32[96]{0:T(128)} %copy-done.78) | copy-start | bytes 1156
  220.2 291.9 %copy-start.81 = (f32[96]{0:T(128)S(1)}, f32[96]{0:T(128)}, u32[]{:S(2)}) copy-start(f32[96]{0:T(128)} %copy-done.80) | copy-start | bytes 1156
  220.3 290.8 %collective-permute-start.6 = (bf16[3,70,96]{1,0,2:T(4,128)(2,1)S(1)}, bf16[3,70,96]{1,0,2:T(4,128)(2,1)S(1)}, u32[]{:S(2)}, u32[]{:S(2)}) collective-permute-start(bf16[3,70,96]{1,0,2:T(4,128)(2,1)S(1)} %get-tuple-element.81), channel_id=1, source_target_pairs={{0,64},{8,72},{16,80},{24,88},{32,96},{40,104},{48,112},{56,120},{... | collective-permute-start | bytes 120968 | tf_op jit(solution)/shard_map/ppermute | solution.py:12
  226.7 284.3 %collective-permute-start.7 = (bf16[3,70,96]{1,0,2:T(4,128)(2,1)S(1)}, bf16[3,70,96]{1,0,2:T(4,128)(2,1)S(1)}, u32[]{:S(2)}, u32[]{:S(2)}) collective-permute-start(bf16[3,70,96]{1,0,2:T(4,128)(2,1)S(1)} %get-tuple-element.82), channel_id=1, source_target_pairs={{64,0},{72,8},{80,16},{88,24},{96,32},{104,40},{112,48},{120,56},{... | collective-permute-start | bytes 120968 | tf_op jit(solution)/shard_map/ppermute | solution.py:12
  (47 other events, 2227.8 us)
Sparse Core Ops, SparseCore 0:
  123.1 49.5 reduce-scatter.8
  175.5 42.9 reduce-scatter.6
Sparse Core Ops, SparseCore 1:
  130.4 574.7 all-reduce.4
where the time goes:
time: 717 us; the launch traced here: 716 us
  blocking collectives  374 us (52%)
  waiting for transfers between devices  231 us (32%)
  other arithmetic  46.2 us (6%)
  starting transfers between devices  26 us (4%)
  between operations  17.1 us (2%)
  local copies, waits for them, and re-layouts  16.4 us (2%)
    psum x1, blocking collectives, shards(): lax.psum((grad_in, grad_out, grad_kernel), 'sp')  282 us
    psum x1, waiting for transfers between devices, shards(): lax.psum((grad_in, grad_out, grad_kernel), 'sp')  180 us
    unnamed x5, waiting for transfers between devices  50.4 us
    all_gather x1, blocking collectives, shards(): grad_all = lax.all_gather(grad_map, 'ch', axis=2, tiled=True)  29.8 us
    all_gather x1, blocking collectives, shards(): lax.all_gather(((conv_f - mean) * rstd).astype(jnp.bfloat16), 'ch', axis=...  29.7 us
    ppermute x8, starting transfers between devices, passed_along(): return lax.ppermute(block, axis, route)  25.8 us
    reduce_sum x3, other arithmetic, shards(): jnp.sum(d_conv_f * padded[row:row + rows, col:col + cols], axis=(0, 1))  18.2 us
    psum x1, blocking collectives, shards(): lax.psum((jnp.sum(d_norm, axis=-1, keepdims=True), jnp.sum(d_norm * local...  16.5 us
  transfers between devices with their start and end apart: 11, of which 4 were waited for; matrix products, arithmetic and copies ran while one was open for 6% of the time, Pallas kernels for 0%

commit v1 on v0

--- a/solution.py
+++ b/solution.py
@@ -48,8 +48,9 @@
     mean = first_sum / chans
     var = square_sum / chans - mean * mean
     rstd = lax.rsqrt(var + 1e-06)
-    normed_all = lax.all_gather(
-        ((conv_f - mean) * rstd).astype(jnp.bfloat16), "ch", axis=2, tiled=True
+    matrix = ((conv_f - mean) * rstd).astype(jnp.bfloat16)
+    normed_all = jnp.concatenate(
+        lax.all_to_all(jnp.stack([matrix for _ in range(lax.axis_size("ch"))], 0), "ch", 0, 0), 2
     )
     local_hat = (conv_f - mean) * rstd
     pre = jnp.einsum("hwc,cf->hwf", normed_all, w_in, preferred_element_type=jnp.float32)

time: 717 us -> 684 us (0.954)
  other arithmetic: 46.2 us -> 7.19 us
  waiting for transfers between devices: 231 us -> 261 us
  blocking collectives: 374 us -> 345 us
  starting transfers between devices: 26 us -> 35.5 us
    all_gather x1 -> x0, blocking collectives: 29.7 us -> none  [shards(): lax.all_gather(((conv_f - mean) * rstd).astype(jnp.bfloat16), 'ch', axis=...]
    reduce_sum x3, other arithmetic: 18.2 us -> 1.05 us  [shards(): jnp.sum(d_conv_f * padded[row:row + rows, col:col + cols], axis=(0, 1))]
    unnamed x5, waiting for transfers between devices: 50.4 us -> 67.2 us
    ppermute x8, waiting for transfers between devices: 0.51 us -> 14.1 us  [passed_along(): return lax.ppermute(block, axis, route)]
    reduce_sum x1, other arithmetic: 12.5 us -> 1 us  [shards(): jnp.sum(conv_f, axis=-1, keepdims=True)]
    broadcast_in_dim x2, other arithmetic: 12.5 us -> 2.15 us  [shards(): return (output[None], grad_image[None], grad_in, grad_out, grad_kernel)]
    all_to_all x0 -> x1, starting transfers between devices: none -> 8.27 us  [shards(): lax.all_to_all(jnp.stack([matrix for _ in range(lax.axis_size('ch'))], 0)...]
  transfers between devices with their start and end apart: 11 -> 12, of which waited for: 4 -> 7; matrix products, arithmetic and copies ran while one was open for 6% -> 2% of each run, Pallas kernels for 0% -> 0%
where the time goes in v1:
time: 684 us
  blocking collectives  345 us (50%)
  waiting for transfers between devices  261 us (38%)
  starting transfers between devices  35.5 us (5%)
  between operations  16.6 us (2%)
  local copies, waits for them, and re-layouts  13.7 us (2%)
  other arithmetic  7.19 us (1%)
    psum x1, blocking collectives, shards(): lax.psum((grad_in, grad_out, grad_kernel), 'sp')  282 us
    psum x1, waiting for transfers between devices, shards(): lax.psum((grad_in, grad_out, grad_kernel), 'sp')  179 us
    unnamed x5, waiting for transfers between devices  67.2 us
    all_gather x1, blocking collectives, shards(): grad_all = lax.all_gather(grad_map, 'ch', axis=2, tiled=True)  30 us
    ppermute x8, starting transfers between devices, passed_along(): return lax.ppermute(block, axis, route)  27.2 us
    psum x1, blocking collectives, shards(): lax.psum((jnp.sum(d_norm, axis=-1, keepdims=True), jnp.sum(d_norm * local...  16.4 us
    psum x1, blocking collectives, shards(): lax.psum((jnp.sum(conv_f, axis=-1, keepdims=True), jnp.sum(conv_f * conv_...  16.1 us
    ppermute x8, waiting for transfers between devices, passed_along(): return lax.ppermute(block, axis, route)  14.1 us
  transfers between devices with their start and end apart: 12, of which 7 were waited for; matrix products, arithmetic and copies ran while one was open for 2% of the time, Pallas kernels for 0%

profile of v1, /device:TPU:6, one launch (start us, length us, event | category | flops | bytes accessed | tf_op | source)
XLA Modules:
  0.0 683.6 jit_solution(18026066354694282077)
XLA Ops:
  8.0 0.8 fusion.126
  8.8 1.7 collective-permute-start
  10.5 1.3 collective-permute-start.1
  11.8 0.7 convert_element_type.55
  12.8 2.2 collective-permute-done.1
  15.0 0.9 pad_maximum_fusion
  15.9 9.7 %collective-permute-start.2 = (bf16[3,70,96]{2,1,0:T(8,128)(2,1)S(1)}, bf16[3,70,96]{2,1,0:T(8,128)(2,1)S(1)}, u32[]{:S(2)}, u32[]{:S(2)}) collective-permute-start(bf16[3,70,96]{2,1,0:T(8,128)(2,1)S(1)} %get-tuple-element.68), channel_id=1, source_target_pairs={{0,64},{8,72},{16,80},{24,88},{32,96},{40,104},{48,112},{56,120},{... | collective-permute-start | bytes 120968 | tf_op jit(solution)/shard_map/ppermute | solution.py:12
  25.5 1.3 collective-permute-start.3
  27.0 0.4 collective-permute-done.2
  27.3 8.2 %collective-permute-done.3 = bf16[3,70,96]{2,1,0:T(8,128)(2,1)S(1)} collective-permute-done((bf16[3,70,96]{2,1,0:T(8,128)(2,1)S(1)}, bf16[3,70,96]{2,1,0:T(8,128)(2,1)S(1)}, u32[]{:S(2)}, u32[]{:S(2)}) %collective-permute-start.3) | collective-permute-done | bytes 40352 | tf_op jit(solution)/shard_map/ppermute | solution.py:12
  35.5 0.9 maximum_convert_fusion
  36.5 1.0 convert_reduce_fusion.1
  37.6 16.1 %all-reduce.2 = (f32[4,64,1]{1,0,2:T(4,128)S(1)}, f32[4,64,1]{1,0,2:T(4,128)S(1)}) all-reduce(f32[4,64,1]{1,0,2:T(4,128)S(1)} %bitcast.206, f32[4,64,1]{1,0,2:T(4,128)S(1)} %bitcast.205), channel_id=1, replica_groups=mesh['sp'=64,'ch'=8] {'ch'}, use_global_device_ids=true, to_apply=%region_3.4 | all-reduce | flops 512 | bytes 4096 | tf_op jit(solution)/shard_map/psum | solution.py:44
  53.9 0.9 stack.161
  54.8 8.3 %all-to-all-start = ((bf16[8,4,64,96]{3,2,1,0:T(8,128)(2,1)}), bf16[8,4,64,96]{3,2,1,0:T(8,128)(2,1)S(1)}, u32[]{:S(2)}, u32[]{:S(2)}) async-start(bf16[8,4,64,96]{3,2,1,0:T(8,128)(2,1)} %stack.161), calls=%async_computation | async-start | bytes 1048576 | tf_op jit(solution)/shard_map/all_to_all | solution.py:53
  63.2 30.0 %all-gather = bf16[1,4,64,768]{2,1,0,3:T(4,128)(2,1)S(1)} all-gather(bf16[1,4,64,96]{2,1,0,3:T(4,128)(2,1)S(1)} %copy.11), channel_id=2, replica_groups=mesh['sp'=64,'ch'=8] {'ch'}, dimensions={3}, use_global_device_ids=true | all-gather | bytes 442368 | tf_op jit(solution)/shard_map/all_gather | solution.py:65
  93.2 0.5 copy.12
  93.8 0.3 copy.10
  94.1 0.4 reshape.22
  94.6 0.4 fusion.4
  95.2 0.4 fusion
  95.6 0.7 copy-done.2
  96.3 0.4 convolution_convert_fusion
  96.7 0.6 copy.15
  97.2 1.2 reshape.33
  98.6 1.4 convolution_convert_fusion.1
  100.0 0.6 copy.13
  100.6 1.2 reshape.31
  101.9 1.4 convolution_bitcast_fusion.1
  103.4 1.4 convolution_bitcast_fusion
  104.8 39.9 %reduce-scatter.9.cloned.1.call-done = bf16[96,256]{1,0:T(8,128)(2,1)} async-done(((bf16[768,256]{1,0:T(8,128)(2,1)}), bf16[96,256]{1,0:T(8,128)(2,1)}) %reduce-scatter.9.cloned.1.call-update) | async-done | bytes 49168
  144.7 0.9 reshape.34
  145.9 16.4 %all-reduce.1 = (f32[4,64]{1,0:T(4,128)S(1)}, f32[4,64,1]{1,0,2:T(4,128)S(1)}) all-reduce(f32[4,64]{1,0:T(4,128)S(1)} %get-tuple-element.55, f32[4,64,1]{1,0,2:T(4,128)S(1)} %bitcast.207), channel_id=1, replica_groups=mesh['sp'=64,'ch'=8] {'ch'}, use_global_device_ids=true, to_apply=%region_9.10 | all-reduce | flops 512 | bytes 4096 | tf_op jit(solution)/shard_map/psum | solution.py:79
  162.3 27.3 %reduce-scatter.7.cloned.1.call-done = bf16[96,256]{1,0:T(8,128)(2,1)} async-done(((bf16[768,256]{1,0:T(8,128)(2,1)}), bf16[96,256]{1,0:T(8,128)(2,1)}) %reduce-scatter.7.cloned.1.call-update) | async-done | bytes 49168
  189.6 0.9 reshape.32
  190.6 0.5 fusion.68
  191.1 1.3 collective-permute-start.4
  192.4 0.7 fusion.120
  193.1 0.3 fusion.69
  193.4 1.3 collective-permute-start.5
  194.7 3.4 collective-permute-done.5
  198.2 9.4 %collective-permute-start.6 = (bf16[3,70,96]{2,1,0:T(8,128)(2,1)S(1)}, bf16[3,70,96]{2,1,0:T(8,128)(2,1)S(1)}, u32[]{:S(2)}, u32[]{:S(2)}) collective-permute-start(bf16[3,70,96]{2,1,0:T(8,128)(2,1)S(1)} %get-tuple-element.66), channel_id=1, source_target_pairs={{0,64},{8,72},{16,80},{24,88},{32,96},{40,104},{48,112},{56,120},{... | collective-permute-start | bytes 120968 | tf_op jit(solution)/shard_map/ppermute | solution.py:12
  207.8 1.3 collective-permute-start.7
  209.5 282.1 %psum.55 = f32[7,7,96]{2,1,0:T(8,128)} all-reduce(f32[7,7,96]{2,1,0:T(8,128)S(1)} %reshape.23), channel_id=1, replica_groups=mesh['sp'=64,'ch'=8] {'sp'}, use_global_device_ids=true, to_apply=%region_61.62 | all-reduce | flops 4704 | bytes 37632 | tf_op jit(solution)/shard_map/psum | solution.py:102
  491.9 1.5 fusion.121
  493.4 179.2 %all-reduce.5.cloned.1.call-done = (f32[768,384]{1,0:T(8,128)}, f32[384,768]{1,0:T(8,128)}) async-done(((f32[768,384]{1,0:T(8,128)}, f32[384,768]{1,0:T(8,128)}), (f32[768,384]{1,0:T(8,128)}, f32[384,768]{1,0:T(8,128)})) %all-reduce.5.cloned.1.call-update) | async-done | bytes 2359312 | tf_op jit(solution)/shard_map/psum | solution.py:102
  672.7 2.5 copy.19
  675.1 1.0 copy.20
  (146 shorter events, 2.0 us)
Async XLA Ops:
  8.0 86.5 %copy-start = (bf16[768,384]{1,0:T(8,128)(2,1)S(1)}, bf16[768,384]{1,0:T(8,128)(2,1)}, u32[]{:S(2)}) copy-start(bf16[768,384]{1,0:T(8,128)(2,1)} %param.8) | copy-start | bytes 1769476
  8.8 3.9 collective-permute-start
  10.5 4.4 collective-permute-start.1
  12.6 23.8 %copy-start.7 = (f32[96]{0:T(128)}, f32[96]{0:T(128)S(1)}, u32[]{:S(2)}) copy-start(f32[96]{0:T(128)S(1)} %get-tuple-element.79) | copy-start | bytes 1156
  12.6 23.8 %copy-start.9 = (f32[96]{0:T(128)}, f32[96]{0:T(128)S(1)}, u32[]{:S(2)}) copy-start(f32[96]{0:T(128)S(1)} %get-tuple-element.80) | copy-start | bytes 1156
  12.6 23.8 %copy-start.11 = (f32[96]{0:T(128)}, f32[96]{0:T(128)S(1)}, u32[]{:S(2)}) copy-start(f32[96]{0:T(128)S(1)} %get-tuple-element.81) | copy-start | bytes 1156
  12.6 23.8 %copy-start.13 = (f32[96]{0:T(128)}, f32[96]{0:T(128)S(1)}, u32[]{:S(2)}) copy-start(f32[96]{0:T(128)S(1)} %get-tuple-element.82) | copy-start | bytes 1156
  12.6 23.8 %copy-start.15 = (f32[96]{0:T(128)}, f32[96]{0:T(128)S(1)}, u32[]{:S(2)}) copy-start(f32[96]{0:T(128)S(1)} %get-tuple-element.83) | copy-start | bytes 1156
  12.6 23.8 %copy-start.17 = (f32[96]{0:T(128)}, f32[96]{0:T(128)S(1)}, u32[]{:S(2)}) copy-start(f32[96]{0:T(128)S(1)} %get-tuple-element.84) | copy-start | bytes 1156
  12.6 23.8 %copy-start.19 = (f32[96]{0:T(128)}, f32[96]{0:T(128)S(1)}, u32[]{:S(2)}) copy-start(f32[96]{0:T(128)S(1)} %get-tuple-element.85) | copy-start | bytes 1156
  12.7 23.8 %copy-start.21 = (f32[96]{0:T(128)}, f32[96]{0:T(128)S(1)}, u32[]{:S(2)}) copy-start(f32[96]{0:T(128)S(1)} %get-tuple-element.86) | copy-start | bytes 1156
  12.7 23.8 %copy-start.23 = (f32[96]{0:T(128)}, f32[96]{0:T(128)S(1)}, u32[]{:S(2)}) copy-start(f32[96]{0:T(128)S(1)} %get-tuple-element.87) | copy-start | bytes 1156
  15.9 11.5 %collective-permute-start.2 = (bf16[3,70,96]{2,1,0:T(8,128)(2,1)S(1)}, bf16[3,70,96]{2,1,0:T(8,128)(2,1)S(1)}, u32[]{:S(2)}, u32[]{:S(2)}) collective-permute-start(bf16[3,70,96]{2,1,0:T(8,128)(2,1)S(1)} %get-tuple-element.68), channel_id=1, source_target_pairs={{0,64},{8,72},{16,80},{24,88},{32,96},{40,104},{48,112},{56,120},{... | collective-permute-start | bytes 120968 | tf_op jit(solution)/shard_map/ppermute | solution.py:12
  25.5 10.0 %collective-permute-start.3 = (bf16[3,70,96]{2,1,0:T(8,128)(2,1)S(1)}, bf16[3,70,96]{2,1,0:T(8,128)(2,1)S(1)}, u32[]{:S(2)}, u32[]{:S(2)}) collective-permute-start(bf16[3,70,96]{2,1,0:T(8,128)(2,1)S(1)} %get-tuple-element.69), channel_id=1, source_target_pairs={{64,0},{72,8},{80,16},{88,24},{96,32},{104,40},{112,48},{120,56},{... | collective-permute-start | bytes 120968 | tf_op jit(solution)/shard_map/ppermute | solution.py:12
  37.6 25.5 %copy-start.6 = (bf16[1,4,64,96]{3,2,1,0:T(8,128)(2,1)S(1)}, bf16[1,4,64,96]{3,2,1,0:T(8,128)(2,1)}, u32[]{:S(2)}) copy-start(bf16[1,4,64,96]{3,2,1,0:T(8,128)(2,1)} %param.6) | copy-start | bytes 147460
  54.8 38.9 %all-to-all-start = ((bf16[8,4,64,96]{3,2,1,0:T(8,128)(2,1)}), bf16[8,4,64,96]{3,2,1,0:T(8,128)(2,1)S(1)}, u32[]{:S(2)}, u32[]{:S(2)}) async-start(bf16[8,4,64,96]{3,2,1,0:T(8,128)(2,1)} %stack.161), calls=%async_computation | async-start | bytes 1048576 | tf_op jit(solution)/shard_map/all_to_all | solution.py:53
  63.1 81.5 %reduce-scatter.9.cloned.1.call-start = ((), (), s32[]{:S(2)}) async-start(), calls=%async_computation.4 | async-start | bytes 442368
  98.5 91.1 %reduce-scatter.7.cloned.1.call-start = ((), (), s32[]{:S(2)}) async-start(), calls=%async_computation.3 | async-start | bytes 442368
  101.9 570.8 %all-reduce.5.cloned.1.call-start = ((), (), s32[]{:S(2)}) async-start(), calls=%async_computation.5 | async-start | bytes 4718592 | tf_op jit(solution)/shard_map/psum | solution.py:102
  191.1 3.6 collective-permute-start.4
  193.4 4.7 collective-permute-start.5
  198.2 293.4 %collective-permute-start.6 = (bf16[3,70,96]{2,1,0:T(8,128)(2,1)S(1)}, bf16[3,70,96]{2,1,0:T(8,128)(2,1)S(1)}, u32[]{:S(2)}, u32[]{:S(2)}) collective-permute-start(bf16[3,70,96]{2,1,0:T(8,128)(2,1)S(1)} %get-tuple-element.66), channel_id=1, source_target_pairs={{0,64},{8,72},{16,80},{24,88},{32,96},{40,104},{48,112},{56,120},{... | collective-permute-start | bytes 120968 | tf_op jit(solution)/shard_map/ppermute | solution.py:12
  207.5 284.1 %copy-start.8 = (f32[96]{0:T(128)S(1)}, f32[96]{0:T(128)}, u32[]{:S(2)}) copy-start(f32[96]{0:T(128)} %copy-done.7) | copy-start | bytes 1156
  207.6 284.1 %copy-start.10 = (f32[96]{0:T(128)S(1)}, f32[96]{0:T(128)}, u32[]{:S(2)}) copy-start(f32[96]{0:T(128)} %copy-done.9) | copy-start | bytes 1156
  207.6 284.1 %copy-start.12 = (f32[96]{0:T(128)S(1)}, f32[96]{0:T(128)}, u32[]{:S(2)}) copy-start(f32[96]{0:T(128)} %copy-done.11) | copy-start | bytes 1156
  207.6 284.1 %copy-start.14 = (f32[96]{0:T(128)S(1)}, f32[96]{0:T(128)}, u32[]{:S(2)}) copy-start(f32[96]{0:T(128)} %copy-done.13) | copy-start | bytes 1156
  207.6 284.1 %copy-start.16 = (f32[96]{0:T(128)S(1)}, f32[96]{0:T(128)}, u32[]{:S(2)}) copy-start(f32[96]{0:T(128)} %copy-done.15) | copy-start | bytes 1156
  207.6 284.1 %copy-start.18 = (f32[96]{0:T(128)S(1)}, f32[96]{0:T(128)}, u32[]{:S(2)}) copy-start(f32[96]{0:T(128)} %copy-done.17) | copy-start | bytes 1156
  207.6 284.1 %copy-start.20 = (f32[96]{0:T(128)S(1)}, f32[96]{0:T(128)}, u32[]{:S(2)}) copy-start(f32[96]{0:T(128)} %copy-done.19) | copy-start | bytes 1156
  207.6 284.1 %copy-start.22 = (f32[96]{0:T(128)S(1)}, f32[96]{0:T(128)}, u32[]{:S(2)}) copy-start(f32[96]{0:T(128)} %copy-done.21) | copy-start | bytes 1156
  207.6 284.1 %copy-start.24 = (f32[96]{0:T(128)S(1)}, f32[96]{0:T(128)}, u32[]{:S(2)}) copy-start(f32[96]{0:T(128)} %copy-done.23) | copy-start | bytes 1156
  207.6 284.1 %copy-start.26 = (f32[96]{0:T(128)S(1)}, f32[96]{0:T(128)}, u32[]{:S(2)}) copy-start(f32[96]{0:T(128)} %copy-done.25) | copy-start | bytes 1156
  207.7 284.1 %copy-start.28 = (f32[96]{0:T(128)S(1)}, f32[96]{0:T(128)}, u32[]{:S(2)}) copy-start(f32[96]{0:T(128)} %copy-done.27) | copy-start | bytes 1156
  207.7 284.1 %copy-start.30 = (f32[96]{0:T(128)S(1)}, f32[96]{0:T(128)}, u32[]{:S(2)}) copy-start(f32[96]{0:T(128)} %copy-done.29) | copy-start | bytes 1156
  207.7 284.1 %copy-start.32 = (f32[96]{0:T(128)S(1)}, f32[96]{0:T(128)}, u32[]{:S(2)}) copy-start(f32[96]{0:T(128)} %copy-done.31) | copy-start | bytes 1156
  207.7 284.1 %copy-start.34 = (f32[96]{0:T(128)S(1)}, f32[96]{0:T(128)}, u32[]{:S(2)}) copy-start(f32[96]{0:T(128)} %copy-done.33) | copy-start | bytes 1156
  207.7 284.1 %copy-start.36 = (f32[96]{0:T(128)S(1)}, f32[96]{0:T(128)}, u32[]{:S(2)}) copy-start(f32[96]{0:T(128)} %copy-done.35) | copy-start | bytes 1156
  207.7 284.1 %copy-start.38 = (f32[96]{0:T(128)S(1)}, f32[96]{0:T(128)}, u32[]{:S(2)}) copy-start(f32[96]{0:T(128)} %copy-done.37) | copy-start | bytes 1156
  207.7 284.1 %copy-start.40 = (f32[96]{0:T(128)S(1)}, f32[96]{0:T(128)}, u32[]{:S(2)}) copy-start(f32[96]{0:T(128)} %copy-done.39) | copy-start | bytes 1156
  207.7 284.1 %copy-start.42 = (f32[96]{0:T(128)S(1)}, f32[96]{0:T(128)}, u32[]{:S(2)}) copy-start(f32[96]{0:T(128)} %copy-done.41) | copy-start | bytes 1156
  207.7 284.1 %copy-start.44 = (f32[96]{0:T(128)S(1)}, f32[96]{0:T(128)}, u32[]{:S(2)}) copy-start(f32[96]{0:T(128)} %copy-done.43) | copy-start | bytes 1156
  207.7 284.1 %copy-start.46 = (f32[96]{0:T(128)S(1)}, f32[96]{0:T(128)}, u32[]{:S(2)}) copy-start(f32[96]{0:T(128)} %copy-done.45) | copy-start | bytes 1156
  207.8 284.1 %copy-start.48 = (f32[96]{0:T(128)S(1)}, f32[96]{0:T(128)}, u32[]{:S(2)}) copy-start(f32[96]{0:T(128)} %copy-done.47) | copy-start | bytes 1156
  207.8 284.1 %copy-start.50 = (f32[96]{0:T(128)S(1)}, f32[96]{0:T(128)}, u32[]{:S(2)}) copy-start(f32[96]{0:T(128)} %copy-done.49) | copy-start | bytes 1156
  207.8 284.1 %copy-start.52 = (f32[96]{0:T(128)S(1)}, f32[96]{0:T(128)}, u32[]{:S(2)}) copy-start(f32[96]{0:T(128)} %copy-done.51) | copy-start | bytes 1156
  207.8 284.1 %copy-start.54 = (f32[96]{0:T(128)S(1)}, f32[96]{0:T(128)}, u32[]{:S(2)}) copy-start(f32[96]{0:T(128)} %copy-done.53) | copy-start | bytes 1156
  207.8 284.1 %copy-start.56 = (f32[96]{0:T(128)S(1)}, f32[96]{0:T(128)}, u32[]{:S(2)}) copy-start(f32[96]{0:T(128)} %copy-done.55) | copy-start | bytes 1156
  207.8 283.8 %collective-permute-start.7 = (bf16[3,70,96]{2,1,0:T(8,128)(2,1)S(1)}, bf16[3,70,96]{2,1,0:T(8,128)(2,1)S(1)}, u32[]{:S(2)}, u32[]{:S(2)}) collective-permute-start(bf16[3,70,96]{2,1,0:T(8,128)(2,1)S(1)} %get-tuple-element.67), channel_id=1, source_target_pairs={{64,0},{72,8},{80,16},{88,24},{96,32},{104,40},{112,48},{120,56},{... | collective-permute-start | bytes 120968 | tf_op jit(solution)/shard_map/ppermute | solution.py:12
  (21 other events, 241.6 us)
Sparse Core Ops, SparseCore 0:
  98.6 45.9 reduce-scatter.8
  147.5 42.1 reduce-scatter.6
Sparse Core Ops, SparseCore 1:
  105.9 566.7 all-reduce.4
